TPU v7x, 256 devices: a whole 4x4x8 slice. The times are simulated.
256 devices in a mesh: tp: 32 (over x, z), dp: 8 (over y, core).
Axes of the slice: x: 4, y: 4, z: 8, core: 2. Of those that a mesh axis runs over, the one named last changes fastest.
Arguments:
- hidden: bfloat16 [32768, 1600], P(('dp', 'tp')), parts along dimension 0
- gain: bfloat16 [1600], replicated, may hold values from 0.5 to 1.5
- head: bfloat16 [1600, 32000], P(None, 'tp')
- lengths: int32 [128], P('dp'), parts along dimension 0, may hold values from 64 to 256, as said below
- mask: int32 [32768], P(('dp', 'tp')), parts along dimension 0, may hold values 0 or 1
- targets: int32 [32768], P(('dp', 'tp')), parts along dimension 0, may hold values from 0 to 31999
Outputs:
- logprob: float32 [32768], P(('dp', 'tp')), parts along dimension 0
- entropy: float32 [32768], P(('dp', 'tp')), parts along dimension 0
There are 8 independent parts, one for each index of `dp`. A program takes and returns all parts, laid end to end along the dimension named above; an argument that names none is the same for every part. Nothing has to cross between parts.
Inputs may be any that keep to these rules, and one draw needn't show every extreme that they name: `lengths`: each sequence's live length; the longest sequence of a batch fills all 256 slots.
All inputs are finite; a program needn't handle non-finite values. No bound on the sum of `mask` on one device may be relied on, other than what follows from the above.
Results may differ from a plain program's by a relative error of at most 0.003.
The roundings to bfloat16 on the way count: a program that leaves them out, or rounds other values in their place, can miss the bound.
Values may be sent and summed in bfloat16 or wider, within the bound.
A program may use at most 128 MiB of HBM per device.

v0:
```python
import jax
import jax.numpy as jnp
from jax import lax
from jax.sharding import PartitionSpec as P

SEQ_LEN = 256


EPS = 1e-06


def on_device(hidden, gain, head, lengths, mask, targets):
    rows = hidden.shape[0]
    width = head.shape[1]
    me = lax.axis_index("tp")
    xf = hidden.astype(jnp.float32)
    meansq = jnp.mean(xf * xf, axis=-1, keepdims=True)
    normed = (xf * lax.rsqrt(meansq + EPS) * gain.astype(jnp.float32)).astype(jnp.bfloat16)
    col_start = me * width
    col_ids = jnp.arange(width, dtype=jnp.int32)
    piece_rows = lax.all_gather(normed, "tp", axis=0, tiled=True)
    piece_tgt = lax.all_gather(targets, "tp", axis=0, tiled=True)
    logits = jnp.dot(piece_rows, head, preferred_element_type=jnp.float32)
    top = jnp.max(logits, axis=-1)
    shifted = logits - top[:, None]
    expo = jnp.exp(shifted)
    sums = jnp.sum(expo, axis=-1)
    ent = jnp.sum(expo * shifted, axis=-1)
    local_id = piece_tgt - col_start
    hit = col_ids[None, :] == local_id[:, None]
    tgt = jnp.sum(jnp.where(hit, logits, 0.0), axis=-1)
    fresh = (top, sums, tgt, ent)
    top, sums, tgt, ent = tuple((new for new in fresh))
    glob_top = lax.pmax(top, "tp")
    scale = jnp.exp(top - glob_top)
    all_sums, all_tgt, all_ent = lax.psum(
        (sums * scale, tgt, (ent + (top - glob_top) * sums) * scale), "tp"
    )
    own_sums = lax.dynamic_slice_in_dim(all_sums, me * rows, rows)
    own_tgt = lax.dynamic_slice_in_dim(all_tgt, me * rows, rows)
    own_ent = lax.dynamic_slice_in_dim(all_ent, me * rows, rows)
    own_top = lax.dynamic_slice_in_dim(glob_top, me * rows, rows)
    log_total = jnp.log(own_sums)
    logp = own_tgt - (own_top + log_total)
    entropy = log_total - own_ent / own_sums
    row_ids = me * rows + jnp.arange(rows, dtype=jnp.int32)
    slot = row_ids % SEQ_LEN
    seq_id = row_ids // SEQ_LEN
    seq_count = lengths.shape[0]
    match = seq_id[:, None] == jnp.arange(seq_count, dtype=jnp.int32)[None, :]
    seq_len = jnp.sum(jnp.where(match, lengths[None, :], 0), axis=1)
    valid = (slot < seq_len) & (mask == 1)
    zero = jnp.zeros_like(logp)
    return (jnp.where(valid, logp, zero), jnp.where(valid, entropy, zero))


def solution(mesh):
    return jax.shard_map(
        on_device,
        mesh=mesh,
        in_specs=(
            P(("dp", "tp"), None),
            P(),
            P(None, "tp"),
            P("dp"),
            P(("dp", "tp")),
            P(("dp", "tp")),
        ),
        out_specs=(P(("dp", "tp")), P(("dp", "tp"))),
        check_vma=False,
    )
```

profile of v0, /device:TPU:8, one launch (start us, length us, event | category | flops | bytes accessed | tf_op | source)
XLA Modules:
  0.0 457.1 jit_solution(10889770379145674299)
XLA Ops:
  7.2 0.0 copy-start
  7.2 0.0 all-gather.3.cloned.1.call-start
  7.2 0.8 convert_element_type.10
  8.1 1.3 fusion.1
  9.4 2.0 fusion.3
  11.4 0.0 all-gather.3.cloned.1.call-update
  11.5 41.9 %all-gather = s32[32,1,128]{2,1,0:T(1,128)S(1)} all-gather(s32[1,1,128]{2,1,0:T(1,128)} %bitcast.8), channel_id=1, replica_groups=mesh['tp'=32,'dp'=8] {'tp'}, dimensions={0}, use_global_device_ids=true | all-gather | bytes 16896 | tf_op jit(solution)/shard_map/all_gather | solution.py:22
  53.3 0.7 select_reduce_fusion.1
  54.1 88.6 %all-gather.3.cloned.1.call-done = bf16[4096,1600]{0,1:T(8,128)(2,1)} async-done(((bf16[128,1600]{0,1:T(8,128)(2,1)}), bf16[4096,1600]{0,1:T(8,128)(2,1)}) %all-gather.3.cloned.1.call-update) | async-done | bytes 13107216 | tf_op jit(solution)/shard_map/all_gather | solution.py:21
  142.7 0.0 copy-done
  142.7 19.6 %fusion.4 = (f32[4096]{0:T(1024)S(1)}, f32[4096,1000]{0,1:T(8,128)}) fusion(bf16[4096,1600]{0,1:T(8,128)(2,1)} %all-gather.3.cloned.1.call-done, bf16[1600,1000]{1,0:T(8,128)(2,1)S(1)} %copy-done), kind=kOutput, calls=%fused_computation.25 | convolution fusion | flops 13111291904 | bytes 32707584 | tf_op jit(solution)/shard_map/dot_general | solution.py:23
  162.3 0.0 copy-start.1
  162.3 140.4 %pmax.7 = f32[4096]{0:T(1024)S(1)} all-reduce(f32[4096]{0:T(1024)S(1)} %get-tuple-element.12), channel_id=1, replica_groups=mesh['tp'=32,'dp'=8] {'tp'}, use_global_device_ids=true, to_apply=%region_5.6 | all-reduce | flops 4096 | bytes 32768 | tf_op jit(solution)/shard_map/pmax | solution.py:34
  302.7 8.6 %fusion = (f32[4096]{0:T(1024)S(1)}, f32[4096]{0:T(1024)S(1)}, f32[4096]{0:T(1024)S(1)}) fusion(f32[4096,1000]{0,1:T(8,128)} %get-tuple-element.13, f32[4096]{0:T(1024)S(1)} %get-tuple-element.12, s32[4096]{0:T(1024)S(1)} %bitcast.6), kind=kLoop, calls=%fused_computation.2 | loop fusion | flops 28659712 | bytes 16465920 | tf_op jit(solution)/shard_map/reduce_sum | solution.py:28
  311.3 137.7 %all-reduce = (f32[4096]{0:T(1024)S(1)}, f32[4096]{0:T(1024)S(1)}, f32[4096]{0:T(1024)S(1)}) all-reduce(f32[4096]{0:T(1024)S(1)} %get-tuple-element.4, f32[4096]{0:T(1024)S(1)} %get-tuple-element.11, f32[4096]{0:T(1024)S(1)} %get-tuple-element.10), channel_id=1, replica_groups=mesh['tp'=32,'dp'=8] {'tp'}, use_global_device_ids=true, to_apply=%region_3.0 | all-reduce | flops 12288 | bytes 98304 | tf_op jit(solution)/shard_map/psum | solution.py:36
  449.0 0.0 copy-done.1
  449.1 0.6 subtract_select_fusion
  449.6 0.6 subtract_select_fusion.1
  (4 shorter events, 0.0 us)
Async XLA Ops:
  7.2 135.6 %copy-start = (bf16[1600,1000]{1,0:T(8,128)(2,1)S(1)}, bf16[1600,1000]{1,0:T(8,128)(2,1)}, u32[]{:S(2)}) copy-start(bf16[1600,1000]{1,0:T(8,128)(2,1)} %param.8) | copy-start | bytes 9600004
  7.2 135.6 %all-gather.3.cloned.1.call-start = ((), (), s32[]{:S(2)}) async-start(), calls=%async_computation | async-start | bytes 13516800 | tf_op jit(solution)/shard_map/all_gather | solution.py:21
  162.3 286.7 %copy-start.1 = (s32[128]{0:T(128)S(1)}, s32[128]{0:T(128)}, u32[]{:S(2)}) copy-start(s32[128]{0:T(128)} %param.10) | copy-start | bytes 1540
Sparse Core Ops, SparseCore 0:
  11.6 131.1 all-gather.2
where the time goes:
time: 457 us
  blocking collectives  320 us (70%)
  waiting for transfers between devices  88.7 us (19%)
  matrix products  19.6 us (4%)
  other arithmetic  14.7 us (3%)
  between operations  14.1 us (3%)
    pmax x1, blocking collectives, on_device(): glob_top = lax.pmax(top, 'tp')  140 us
    psum x1, blocking collectives, on_device(): lax.psum((sums * scale, tgt, (ent + (top - glob_top) * sums) * scale), 'tp')  138 us
    all_gather x1, waiting for transfers between devices, on_device(): piece_rows = lax.all_gather(normed, 'tp', axis=0, tiled=True)  88.6 us
    all_gather x1, blocking collectives, on_device(): piece_tgt = lax.all_gather(targets, 'tp', axis=0, tiled=True)  41.9 us
    dot_general x1, matrix products, on_device(): logits = jnp.dot(piece_rows, head, preferred_element_type=jnp.float32)  19.6 us
  transfers between devices with their start and end apart: 1, of which 1 were waited for; matrix products, arithmetic and copies ran while one was open for 0% of the time, Pallas kernels for 0%

commit v1 on v0

v1 whole, which is shorter than its diff:
```python
import functools

import jax
import jax.numpy as jnp
from jax import lax
from jax.experimental import pallas as pl
from jax.experimental.pallas import tpu as pltpu
from jax.sharding import PartitionSpec as P

SEQ_LEN = 256
EPS = 1e-06

NX, NY, NZ = 4, 4, 8
D = 1600
DE = 1664
ROWS = 128
WIDTH = 1000
TILES = 8
LAST = WIDTH - 7 * 128
SUB = D // 2
HALF = ROWS // 2
GROUP = 256
MESH = pl.DeviceIdType.MESH

PLACE = {1: 0, 7: 1, 2: 2, 6: 3, 3: 4, 5: 5, 0: 6, 4: 7}

X_SEQ = (
    ((1, 0, 0), (1, 0, 1), (1, 1, 0), (1, 1, 1), (3, 0, 0), (3, 0, 1)),
    ((2, 1, 0), (2, 1, 1), (2, 0, 0), (2, 0, 1), (3, 1, 0), (3, 1, 1)),
)
Y_SEQ = (
    ((1, 0, 0), (1, 0, 1), (2, 0, 0), (2, 0, 1), (3, 0, 0), (3, 0, 1)),
    ((2, 1, 0), (2, 1, 1), (1, 1, 0), (1, 1, 1), (3, 1, 0), (3, 1, 1)),
)
Z_SEQ = (
    ((1, 0), (1, 1), (2, 0), (2, 1), (3, 0), (3, 1), (4, 0)),
    ((7, 0), (7, 1), (6, 0), (6, 1), (5, 0), (5, 1), (4, 1)),
)


def unit_of(n, h):
    p = jnp.where(n < 4, -1, (n - 4) // 2)
    u = jnp.where(n < 4, n, (n - 4) % 2)
    other = 1 - h
    shard = jnp.where(p < 0, 0, jnp.where((p == 3) | (p == 5), 3, jnp.where(p == 4, 2 - u, 1 + u)))
    mine = (p == 0) | (p == 1) | (p == 3)
    low = jnp.where(p == 1, 1 - u, u)
    k = jnp.where(p < 0, u, 2 * jnp.where(mine, h, other) + low)
    return shard, k


def compute_step(tok, hb, tb, mx, sm, en, tg, row0, shard, k, col0, first):
    row0 = pl.multiple_of(row0, GROUP)
    rows = pl.ds(row0, GROUP)
    left = tok[rows, :D]
    right = jnp.concatenate([hb[shard, 2 * k], hb[shard, 2 * k + 1]], axis=1)
    logits = jnp.dot(left, right, preferred_element_type=jnp.float32)
    l0, l1 = logits[:, :128], logits[:, 128:]
    lane = lax.broadcasted_iota(jnp.int32, (GROUP, 128), 1)
    inside = lane < jnp.where(k == 3, LAST, 128)
    aim = tb[rows, :]
    base = col0.astype(jnp.float32)
    t = tg[rows, :]
    t = jnp.where(aim == base, l0, t)
    t = jnp.where((aim == base + 128.0) & inside, l1, t)
    tg[rows, :] = t
    l1 = jnp.where(inside, l1, l0)
    old = jnp.where(first, l0, mx[rows, :])
    new = jnp.maximum(jnp.maximum(l0, l1), old)
    d0, d1, da = l0 - new, l1 - new, old - new
    e0, e1, a = jnp.exp(d0), jnp.where(inside, jnp.exp(d1), 0.0), jnp.exp(da)
    s = sm[rows, :]
    en[rows, :] = (en[rows, :] + da * s) * a + (e0 * d0 + e1 * d1)
    sm[rows, :] = s * a + (e0 + e1)
    mx[rows, :] = new


def aim_rows(tok, tb, row0, count):
    ids = tok[pl.ds(row0, count), pl.ds(D, DE - D)].astype(jnp.float32)
    value = ids[:, 0:1] * 256.0 + ids[:, 1:2]
    lane = lax.broadcasted_iota(jnp.int32, (count, 128), 1).astype(jnp.float32)
    tb[pl.ds(row0, count), :] = value - lane


def block_stats(mx, sm, en, tg, row0):
    rows = pl.ds(row0, ROWS)
    m, s, e = mx[rows, :].T, sm[rows, :].T, en[rows, :].T
    top = jnp.max(m, axis=0, keepdims=True)
    gap = m - top
    scale = jnp.exp(gap)
    total = jnp.sum(s * scale, axis=0, keepdims=True)
    ent = jnp.sum((e + gap * s) * scale, axis=0, keepdims=True)
    tgt = jnp.sum(tg[rows, :].T, axis=0, keepdims=True)
    return top, total, ent, tgt


def kernel(
    rows_ref, head_ref, tail_ref, out_ref,
    tok, hb, tb, mx, sm, en, tg, stats, sendbuf, inbox,
    load_sem, xs, xr, ys, yr, zs, zr, bs, br, ss, sr,
):
    tp, dp = lax.axis_index("tp"), lax.axis_index("dp")
    x, z = tp // NZ, tp % NZ
    y, core = dp // 2, dp % 2
    h = y % 2

    def x_peer(step):
        return {"tp": ((x + step) % NX) * NZ + z, "dp": dp}

    def y_peer(step):
        return {"tp": tp, "dp": ((y + step) % NY) * 2 + core}

    def z_peer(step):
        return {"tp": x * NZ + (z + step) % NZ, "dp": dp}

    twin = {"tp": tp, "dp": y * 2 + 1 - core}

    def remote(src, dst, send, recv, peer):
        return pltpu.make_async_remote_copy(
            src_ref=src, dst_ref=dst, send_sem=send, recv_sem=recv, device_id=peer, device_id_type=MESH
        )

    own = PLACE[0] * ROWS
    loads = [pltpu.make_async_copy(rows_ref, tok.at[pl.ds(own, ROWS), :], load_sem.at[8])]
    for t in range(TILES - 1):
        loads.append(pltpu.make_async_copy(head_ref.at[:, pl.ds(t * 128, 128)], hb.at[0, t], load_sem.at[t]))
    loads.append(pltpu.make_async_copy(tail_ref, hb.at[0, TILES - 1], load_sem.at[7]))
    for copy in loads:
        copy.start()

    barrier = pltpu.get_barrier_semaphore()
    peers = [x_peer(1), x_peer(-1), y_peer(1), y_peer(-1), twin] + [z_peer(d) for d in range(1, NZ)]
    for peer in peers:
        pl.semaphore_signal(barrier, inc=1, device_id=peer, device_id_type=MESH)
    pl.semaphore_wait(barrier, len(peers))

    sent = []

    def go(copy):
        copy.start()
        sent.append(copy)

    def piece(shard, tile, sub):
        return hb.at[shard, tile, pl.ds(sub * SUB, SUB), :]

    def place(d, half):
        return tok.at[pl.ds(PLACE[d] * ROWS + half * HALF, HALF), :]

    def tile_of(parity, quarter):
        return (2 * parity + quarter) * 2 + core

    def x_copy(side, i, src_shard):
        shard, quarter, sub = X_SEQ[side][i]
        tile = tile_of(h, quarter)
        return remote(
            piece(src_shard, tile, sub), piece(shard, tile, sub), xs.at[side, i], xr.at[side, i],
            x_peer(-1 if side == 0 else 1),
        )

    def y_copy(side, i, parity):
        shard, quarter, sub = Y_SEQ[side][i]
        tile = tile_of(parity, quarter)
        return remote(
            piece(shard, tile, sub), piece(shard, tile, sub), ys.at[side, i], yr.at[side, i],
            y_peer(-1 if side == 0 else 1),
        )

    def b_copy(kind, i, sender):
        shard, quarter, sub = (X_SEQ + Y_SEQ)[kind][i]
        parity = h if kind < 2 else 1 - h
        tile = (2 * parity + quarter) * 2 + sender
        return remote(piece(shard, tile, sub), piece(shard, tile, sub), bs.at[kind, i], br.at[kind, i], twin)

    def z_copy(side, i, src):
        d, half = Z_SEQ[side][i]
        return remote(
            place(src, half), place(d, half), zs.at[side, i], zr.at[side, i], z_peer(-1 if side == 0 else 1)
        )

    loads[0].wait()
    for i in range(2):
        for side in range(2):
            go(z_copy(side, i, 0))
    for copy in loads[1:]:
        copy.wait()
    for i in range(4):
        for side in range(2):
            go(x_copy(side, i, 0))

    def zero(i, carry):
        rows = pl.ds(pl.multiple_of(i * ROWS, ROWS), ROWS)
        blank = jnp.zeros((ROWS, 128), jnp.float32)
        for ref in (mx, sm, en, tg):
            ref[rows, :] = blank
        return carry

    lax.fori_loop(0, NZ, zero, 0)
    aim_rows(tok, tb, own, ROWS)

    def got_x(i):
        for side in range(2):
            shard, quarter, sub = X_SEQ[side][i]
            x_copy(side, i, 0).wait_recv()
            to = 0 if quarter == 0 else 1
            go(y_copy(to, Y_SEQ[to].index((shard, quarter, sub)), h))
            go(b_copy(side, i, core))
            if i < 2:
                go(x_copy(side, i + 4, shard))

    def got_y(i):
        for side in range(2):
            y_copy(side, i, 1 - h).wait_recv()
            go(b_copy(2 + side, i, core))

    def got_twin(kinds, i):
        for kind in kinds:
            b_copy(kind, i, 1 - core).wait_recv()

    def got_z(i):
        for side in range(2):
            d, half = Z_SEQ[side][i]
            z_copy(side, i, 0).wait_recv()
            if i + 2 < len(Z_SEQ[side]):
                if Z_SEQ[side][i + 2][1] == half:
                    go(z_copy(side, i + 2, d))
            if i == 5 and side == 1:
                go(z_copy(side, 6, d))

    def phase(g0, groups, n0, units):
        def one(i, carry):
            g, n = g0 + i // units, n0 + i % units
            shard, k = unit_of(n, h)
            step = jnp.where(shard == 2, 3, jnp.where(shard == 3, 2, shard))
            col0 = (((x + step) % NX) * NZ + z) * WIDTH + k * 256
            compute_step(tok, hb, tb, mx, sm, en, tg, g * GROUP, shard, k, col0, n == 0)
            return carry

        lax.fori_loop(0, groups * units, one, 0)

    X, Y = (0, 1), (2, 3)
    got_x(0)
    got_z(0)
    got_x(1)
    got_z(1)
    got_y(0)
    aim_rows(tok, tb, 0, GROUP)
    phase(0, 1, 0, 4)
    got_x(2)
    got_twin(X, 0)
    got_twin(X, 1)
    got_z(2)
    phase(0, 1, 4, 2)
    got_y(1)
    got_x(3)
    got_z(3)
    got_y(2)
    aim_rows(tok, tb, GROUP, GROUP)
    phase(1, 1, 0, 6)
    got_x(4)
    got_z(4)
    got_twin(X, 2)
    got_twin(X, 3)
    got_twin(Y, 0)
    got_twin(Y, 1)
    phase(0, 2, 6, 4)
    got_x(5)
    got_z(5)
    got_y(3)
    aim_rows(tok, tb, 2 * GROUP, GROUP)
    phase(2, 1, 0, 10)
    got_y(4)
    got_twin(X, 4)
    got_twin(X, 5)
    got_twin(Y, 2)
    got_twin(Y, 3)
    phase(0, 3, 10, 4)
    got_z(6)
    got_y(5)
    aim_rows(tok, tb, PLACE[4] * ROWS, ROWS)
    phase(3, 1, 0, 14)
    got_twin(Y, 4)
    got_twin(Y, 5)
    phase(0, 4, 14, 2)

    def collect(i, carry):
        parts = block_stats(mx, sm, en, tg, pl.multiple_of(i * ROWS, ROWS))
        for n, part in enumerate(parts):
            stats[i, n:n + 1, :] = part
        return carry

    lax.fori_loop(0, NZ, collect, 0)
    move = pltpu.make_async_copy(stats, sendbuf, load_sem.at[0])
    move.start()
    move.wait()
    for d in range(1, NZ):
        go(remote(sendbuf.at[PLACE[d]], inbox.at[NZ - d], ss.at[d], sr.at[NZ - d], z_peer(d)))
    for d in range(1, NZ):
        remote(sendbuf.at[PLACE[d]], inbox.at[d], ss.at[d], sr.at[d], z_peer(d)).wait_recv()
    all_of = [stats[PLACE[0]]] + [inbox[d] for d in range(1, NZ)]
    top = functools.reduce(jnp.maximum, [part[0:1, :] for part in all_of])
    total = ent = tgt = jnp.zeros((1, ROWS), jnp.float32)
    for part in all_of:
        gap = part[0:1, :] - top
        scale = jnp.exp(gap)
        total += part[1:2, :] * scale
        ent += (part[2:3, :] + gap * part[1:2, :]) * scale
        tgt += part[3:4, :]
    log_total = jnp.log(total)
    out_ref[0:1, :] = tgt - (top + log_total)
    out_ref[1:2, :] = log_total - ent / total
    for copy in sent:
        copy.wait_send()


def on_device(hidden, gain, head, lengths, mask, targets):
    rows = hidden.shape[0]
    me = lax.axis_index("tp")
    xf = hidden.astype(jnp.float32)
    meansq = jnp.mean(xf * xf, axis=-1, keepdims=True)
    normed = (xf * lax.rsqrt(meansq + EPS) * gain.astype(jnp.float32)).astype(jnp.bfloat16)
    ids = jnp.stack([targets // 256, targets % 256], axis=1).astype(jnp.bfloat16)
    wide = jnp.concatenate([normed, ids, jnp.zeros((rows, DE - D - 2), jnp.bfloat16)], axis=1)
    tail = jnp.pad(head[:, 7 * 128:], ((0, 0), (0, 128 - LAST)))
    vm = pltpu.VMEM
    dma = pltpu.SemaphoreType.DMA
    stat = vm((NZ * ROWS, 128), jnp.float32)
    small = vm((NZ, 8, 128), jnp.float32)
    out = pl.pallas_call(
        kernel,
        out_shape=jax.ShapeDtypeStruct((8, ROWS), jnp.float32),
        in_specs=[pl.BlockSpec(memory_space=pl.ANY)] * 3,
        out_specs=pl.BlockSpec(memory_space=pltpu.VMEM),
        scratch_shapes=[
            vm((NZ * ROWS, DE), jnp.bfloat16),
            vm((NX, TILES, D, 128), jnp.bfloat16),
            stat, stat, stat, stat, stat,
            small, small, small,
            dma((9,)),
            dma((2, 6)), dma((2, 6)),
            dma((2, 6)), dma((2, 6)),
            dma((2, 7)), dma((2, 7)),
            dma((4, 6)), dma((4, 6)),
            dma((NZ,)), dma((NZ,)),
        ],
        compiler_params=pltpu.CompilerParams(
            collective_id=0, has_side_effects=True, vmem_limit_bytes=48 << 20
        ),
    )(wide, head, tail)
    row_ids = me * rows + jnp.arange(rows, dtype=jnp.int32)
    slot = row_ids % SEQ_LEN
    seq_id = row_ids // SEQ_LEN
    match = seq_id[:, None] == jnp.arange(lengths.shape[0], dtype=jnp.int32)[None, :]
    seq_len = jnp.sum(jnp.where(match, lengths[None, :], 0), axis=1)
    valid = (slot < seq_len) & (mask == 1)
    return (jnp.where(valid, out[0], 0.0), jnp.where(valid, out[1], 0.0))


def solution(mesh):
    return jax.shard_map(
        on_device,
        mesh=mesh,
        in_specs=(
            P(("dp", "tp"), None),
            P(),
            P(None, "tp"),
            P("dp"),
            P(("dp", "tp")),
            P(("dp", "tp")),
        ),
        out_specs=(P(("dp", "tp")), P(("dp", "tp"))),
        check_vma=False,
    )
```

time: 457 us -> 76.9 us (0.17)
  blocking collectives: 320 us -> 0 us
  waiting for transfers between devices: 88.7 us -> 0 us
  Pallas kernels: 0 us -> 69.1 us
  matrix products: 19.6 us -> 0 us
  between operations: 14.1 us -> 0.72 us
  other arithmetic: 14.7 us -> 2.85 us
    pmax x1 -> x0, blocking collectives: 140 us -> none  [on_device(): glob_top = lax.pmax(top, 'tp')]
    psum x1 -> x0, blocking collectives: 138 us -> none  [on_device(): lax.psum((sums * scale, tgt, (ent + (top - glob_top) * sums) * scale), 'tp')]
    all_gather x1 -> x0, waiting for transfers between devices: 88.6 us -> none  [on_device(): piece_rows = lax.all_gather(normed, 'tp', axis=0, tiled=True)]
    pallas_call x0 -> x1, Pallas kernels: none -> 69.1 us  [on_device(): pl.pallas_call(kernel, out_shape=jax.ShapeDtypeStruct((8, ROWS), jnp.floa...]
    all_gather x1 -> x0, blocking collectives: 41.9 us -> none  [on_device(): piece_tgt = lax.all_gather(targets, 'tp', axis=0, tiled=True)]
    dot_general x1 -> x0, matrix products: 19.6 us -> none  [on_device(): logits = jnp.dot(piece_rows, head, preferred_element_type=jnp.float32)]
    reduce_sum x1 -> x0, other arithmetic: 8.57 us -> none  [on_device(): ent = jnp.sum(expo * shifted, axis=-1)]
  transfers between devices with their start and end apart: 1 -> 0, of which waited for: 1 -> 0; matrix products, arithmetic and copies ran while one was open for 0% -> 0% of each run, Pallas kernels for 0% -> 0%
where the time goes in v1:
time: 76.9 us; the launch traced here: 76.4 us
  Pallas kernels  69.1 us (90%)
  local copies, waits for them, and re-layouts  3.73 us (5%)
  other arithmetic  2.85 us (4%)
    pallas_call x1, Pallas kernels, on_device(): pl.pallas_call(kernel, out_shape=jax.ShapeDtypeStruct((8, ROWS), jnp.floa...  69.1 us
    unnamed x7, local copies, waits for them, and re-layouts  3.23 us

profile of v1, /device:TPU:8, one launch (start us, length us, event | category | flops | bytes accessed | tf_op | source)
XLA Modules:
  0.0 76.4 jit_solution(3194862617624666591)
XLA Ops:
  0.6 0.0 slice-start
  0.6 1.3 %copy.11 = bf16[128,1600]{1,0:T(8,128)(2,1)S(1)} copy(bf16[128,1600]{0,1:T(8,128)(2,1)} %param.6) | data formatting | bytes 819200 | tf_op args[0]
  1.9 0.2 fusion
  2.1 0.7 convert_element_type.13
  2.8 0.2 fusion.2
  3.0 0.7 fusion.4
  3.7 0.1 copy.12
  3.8 0.1 copy.13
  3.9 0.0 copy-start.2
  4.0 0.0 copy-start.1
  4.0 0.1 concatenate.4.rows_ref
  4.1 0.0 slice-done
  4.1 0.1 pad.4.tail_ref
  4.2 0.0 copy-start
  4.2 1.9 %copy-done = bf16[1600,1000]{1,0:T(8,128)(2,1)S(1)} copy-done((bf16[1600,1000]{1,0:T(8,128)(2,1)S(1)}, bf16[1600,1000]{1,0:T(8,128)(2,1)}, u32[]{:S(2)}) %copy-start) | copy-done | bytes 3200024
  6.1 69.1 %shard_map.77 = f32[8,128]{1,0:T(8,128)S(1)} custom-call(bf16[128,1664]{1,0:T(8,128)(2,1)S(1)} %concatenate.4.rows_ref, bf16[1600,1000]{1,0:T(8,128)(2,1)S(1)} %copy-done, bf16[1600,128]{1,0:T(8,128)(2,1)S(1)} %pad.4.tail_ref), custom_call_target="tpu_custom_call" | custom-call | tf_op jit(solution)/shard_map/pallas_call | solution.py:328
  75.3 0.0 copy-done.2
  75.3 0.1 select_reduce_fusion
  75.4 0.0 copy-done.1
  75.4 0.5 bitcast_select_fusion
  75.9 0.5 bitcast_select_fusion.1
  (3 shorter events, 0.0 us)
Async XLA Ops:
  0.6 3.5 %slice-start = ((bf16[1600,1000]{1,0:T(8,128)(2,1)}), bf16[1600,104]{1,0:T(8,128)(2,1)S(1)}, s32[]{:S(2)}) async-start(bf16[1600,1000]{1,0:T(8,128)(2,1)} %head_ref.1), calls=%async_computation | async-start | bytes 819200 | tf_op jit(solution)/shard_map/slice | solution.py:323
  3.9 71.4 %copy-start.2 = (s32[16]{0:T(128)S(1)}, s32[16]{0:T(128)}, u32[]{:S(2)}) copy-start(s32[16]{0:T(128)} %param.9) | copy-start | bytes 196
  4.0 71.5 %copy-start.1 = (s32[128]{0:T(128)S(1)}, s32[128]{0:T(128)}, u32[]{:S(2)}) copy-start(s32[128]{0:T(128)} %param.10) | copy-start | bytes 1540
  4.2 1.9 %copy-start = (bf16[1600,1000]{1,0:T(8,128)(2,1)S(1)}, bf16[1600,1000]{1,0:T(8,128)(2,1)}, u32[]{:S(2)}) copy-start(bf16[1600,1000]{1,0:T(8,128)(2,1)} %head_ref.1) | copy-start | bytes 9600004

commit v2 on v0

v2 whole, which is shorter than its diff:
```python
import functools

import jax
import jax.numpy as jnp
from jax import lax
from jax.experimental import pallas as pl
from jax.experimental.pallas import tpu as pltpu
from jax.sharding import PartitionSpec as P

SEQ_LEN = 256
EPS = 1e-06

NX, NY, NZ = 4, 4, 8
D = 1600
DE = 1664
ROWS = 128
WIDTH = 1000
TILES = 8
LAST = WIDTH - 7 * 128
SUBS = 4
SUB = D // SUBS
HALF = ROWS // 2
MESH = pl.DeviceIdType.MESH

PLACE = {1: 0, 7: 1, 2: 2, 6: 3, 3: 4, 5: 5, 0: 6, 4: 7}

X_SEQ = tuple(
    tuple((shard, quarter, sub) for shard, quarter in seq for sub in range(SUBS))
    for seq in (((1, 0), (1, 1), (3, 0)), ((2, 1), (2, 0), (3, 1)))
)
Y_SEQ = tuple(
    tuple((shard, quarter, sub) for shard, quarter in seq for sub in range(SUBS))
    for seq in (((1, 0), (2, 0), (3, 0)), ((2, 1), (1, 1), (3, 1)))
)
Z_SEQ = (
    ((1, 0), (1, 1), (2, 0), (2, 1), (3, 0), (3, 1), (4, 0)),
    ((7, 0), (7, 1), (6, 0), (6, 1), (5, 0), (5, 1), (4, 1)),
)

QUADS = ((0, 1), (2, 4), (3, 6), (5, 7))
STEPS = (
    ("A", 0, 0), ("A", 1, 0), ("A", 2, 0), ("B", 0, 2), ("B", 0, 4), ("A", 3, 0), ("A", 0, 1), ("A", 3, 1),
    ("A", 4, 0), ("A", 4, 1), ("B", 0, 3), ("B", 1, 3), ("B", 0, 6), ("B", 1, 6), ("A", 5, 0), ("A", 5, 1),
    ("A", 0, 2), ("A", 5, 2), ("B", 0, 5), ("B", 1, 5), ("A", 6, 0), ("A", 6, 1), ("A", 6, 2), ("B", 2, 5),
    ("A", 7, 0), ("A", 7, 1), ("A", 7, 2), ("A", 7, 3), ("B", 2, 7), ("B", 1, 7), ("B", 0, 7), ("A", 0, 3),
)
DONE = {27: (7,), 28: (4, 5), 29: (2, 3), 30: (0, 1)}

TIMES = {"x0": 5.0, "x": 2.22, "z0": 5.5, "z": 4.63, "y": 4.2, "twin": 1.5, "step": 0.81}


def needs(step):
    kind, rows, columns = step
    tokens = rows if kind == "A" else 2 * rows + 2
    wanted = [("z", i) for i in range(tokens)]
    for p in QUADS[columns] if kind == "A" else (columns,):
        if p in (2, 3, 5):
            upto = SUBS * ((2, 3, 5).index(p) + 1)
            wanted += [(s, i) for s in ("x", "tx") for i in range(upto)]
        if p in (4, 6, 7):
            upto = SUBS * ((4, 6, 7).index(p) + 1)
            wanted += [(s, i) for s in ("y", "ty") for i in range(upto)]
    return set(wanted)


def plan():
    at = {}
    for i in range(3 * SUBS):
        at["x", i] = TIMES["x0"] + TIMES["x"] * (i + 1)
        at["y", i] = at["x", i] + TIMES["y"]
        at["tx", i] = at["x", i] + TIMES["twin"]
        at["ty", i] = at["y", i] + TIMES["twin"]
    for i in range(7):
        at["z", i] = TIMES["z0"] + TIMES["z"] * (i + 1)
    left = sorted(at, key=lambda event: (at[event], event))
    now, ahead = TIMES["x0"], []
    for step in STEPS:
        wanted, events = needs(step), []
        while left and (at[left[0]] <= now or wanted & set(left)):
            event = left.pop(0)
            now = max(now, at[event])
            events.append(event)
        ahead.append(events)
        now += TIMES["step"]
    return ahead, left


def packed(i):
    codes = [(0 if kind == "A" else 64) + rows * 8 + columns for kind, rows, columns in STEPS]
    words = [sum(code << (7 * j) for j, code in enumerate(codes[w:w + 4])) for w in range(0, len(codes), 4)]
    word = jnp.int32(words[0])
    for w in range(1, len(words)):
        word = jnp.where(i // 4 == w, jnp.int32(words[w]), word)
    shift = 7 * (i % 4)
    code = lax.shift_right_logical(word, shift) & 127
    return code // 64, (code // 8) % 8, code % 8


def pair_units(p, h):
    mine = (p == 2) | (p == 3) | (p == 5)
    half = jnp.where(mine, h, 1 - h)
    units = []
    for u in range(2):
        crossed = jnp.where(p == 6, 2 - u, 1 + u)
        shard = jnp.where(p < 2, 0, jnp.where((p == 5) | (p == 7), 3, crossed))
        low = jnp.where(p == 3, 1 - u, u)
        units.append((shard, jnp.where(p < 2, 2 * p + u, 2 * half + low)))
    return units


def compute_step(tok, hb, tb, mx, sm, en, tg, spans, units, first):
    def load(ref):
        return jnp.concatenate([ref[rows, :] for rows in spans], axis=0)

    def store(ref, value):
        at = 0
        for rows in spans:
            ref[rows, :] = value[at:at + rows.size, :]
            at += rows.size

    left = jnp.concatenate([tok[rows, :D] for rows in spans], axis=0)
    tiles = [hb[shard, 2 * k + j] for shard, k, _ in units for j in range(2)]
    logits = jnp.dot(left, jnp.concatenate(tiles, axis=1), preferred_element_type=jnp.float32)
    parts = [logits[:, i * 128:(i + 1) * 128] for i in range(len(tiles))]
    lane = lax.broadcasted_iota(jnp.int32, (left.shape[0], 128), 1)
    aim, t = load(tb), load(tg)
    inside = []
    for i, (_, k, col0) in enumerate(units):
        base = col0.astype(jnp.float32)
        within = lane < jnp.where(k == 3, LAST, 128)
        inside += [None, within]
        t = jnp.where(aim == base, parts[2 * i], t)
        t = jnp.where((aim == base + 128.0) & within, parts[2 * i + 1], t)
    store(tg, t)
    parts = [part if within is None else jnp.where(within, part, parts[0]) for part, within in zip(parts, inside)]
    old = load(mx)
    if first is not None:
        old = jnp.where(first, parts[0], old)
    new = functools.reduce(jnp.maximum, parts, old)
    gap = old - new
    scale = jnp.exp(gap)
    s = load(sm)
    total = s * scale
    ent = (load(en) + gap * s) * scale
    for part, within in zip(parts, inside):
        d = part - new
        e = jnp.exp(d)
        if within is not None:
            e = jnp.where(within, e, 0.0)
        total += e
        ent += e * d
    store(mx, new)
    store(sm, total)
    store(en, ent)


def aim_rows(tok, tb, row0, count):
    ids = tok[pl.ds(row0, count), pl.ds(D - 64, 128)].astype(jnp.float32)
    value = ids[:, 64:65] * 256.0 + ids[:, 65:66]
    lane = lax.broadcasted_iota(jnp.int32, (count, 128), 1).astype(jnp.float32)
    tb[pl.ds(row0, count), :] = value - lane


def block_stats(mx, sm, en, tg, stats, block):
    rows = pl.ds(block * ROWS, ROWS)
    m, s, e = mx[rows, :].T, sm[rows, :].T, en[rows, :].T
    top = jnp.max(m, axis=0, keepdims=True)
    gap = m - top
    scale = jnp.exp(gap)
    stats[block, 0:1, :] = top
    stats[block, 1:2, :] = jnp.sum(s * scale, axis=0, keepdims=True)
    stats[block, 2:3, :] = jnp.sum((e + gap * s) * scale, axis=0, keepdims=True)
    stats[block, 3:4, :] = jnp.sum(tg[rows, :].T, axis=0, keepdims=True)


def norm_rows(hid, gain_ref, target_ref, stage):
    total = jnp.zeros((8, ROWS), jnp.float32)
    for i in range(0, D, 160):
        part = hid[i:i + 160, :].astype(jnp.float32)
        total += jnp.sum((part * part).reshape(20, 8, ROWS), axis=0)
    scale = lax.rsqrt(jnp.sum(total, axis=0, keepdims=True) * (1.0 / D) + EPS)
    target = target_ref[...]
    for i in range(0, DE, 128):
        if i + 128 <= D:
            part = hid[i:i + 128, :].astype(jnp.float32) * scale
            gain = gain_ref[:, i:i + 128].astype(jnp.float32)
            stage[:, i:i + 128] = (part.T * gain).astype(jnp.bfloat16)
        else:
            n = D - i
            part = hid[i:D, :].astype(jnp.float32) * scale
            row = lax.broadcasted_iota(jnp.int32, (128 - n, ROWS), 0)
            high = jnp.broadcast_to((target // 256).astype(jnp.float32), row.shape)
            low = jnp.broadcast_to((target % 256).astype(jnp.float32), row.shape)
            more = jnp.where(row == 0, high, jnp.where(row == 1, low, 0.0))
            gain = jnp.concatenate(
                [gain_ref[:, i:D].astype(jnp.float32), jnp.ones((1, 128 - n), jnp.float32)], axis=1
            )
            stage[:, i:i + 128] = (jnp.concatenate([part, more], axis=0).T * gain).astype(jnp.bfloat16)


def kernel(
    hid_ref, gain_ref, target_ref, head_ref, out_ref,
    hid, stage, tail, stage7, tok, hb, tb, mx, sm, en, tg, stats, inbox,
    load_sem, xs, xr, ys, yr, zs, zr, bs, br, ss, sr,
):
    tp, dp = lax.axis_index("tp"), lax.axis_index("dp")
    x, z = tp // NZ, tp % NZ
    y, core = dp // 2, dp % 2
    h = y % 2

    def x_peer(step):
        return {"tp": ((x + step) % NX) * NZ + z, "dp": dp}

    def y_peer(step):
        return {"tp": tp, "dp": ((y + step) % NY) * 2 + core}

    def z_peer(step):
        return {"tp": x * NZ + (z + step) % NZ, "dp": dp}

    twin = {"tp": tp, "dp": y * 2 + 1 - core}

    def remote(src, dst, send, recv, peer):
        return pltpu.make_async_remote_copy(
            src_ref=src, dst_ref=dst, send_sem=send, recv_sem=recv, device_id=peer, device_id_type=MESH
        )

    barrier = pltpu.get_barrier_semaphore()
    peers = [z_peer(d) for d in (4, 3, 5, 2, 6, 1, 7)] + [x_peer(1), x_peer(-1), y_peer(1), y_peer(-1), twin]
    for peer in peers:
        pl.semaphore_signal(barrier, inc=1, device_id=peer, device_id_type=MESH)

    own = PLACE[0] * ROWS
    hid_load = pltpu.make_async_copy(hid_ref, hid, load_sem.at[8])
    tail_load = pltpu.make_async_copy(head_ref.at[:, pl.ds((TILES - 1) * 128, LAST)], tail, load_sem.at[7])
    tile_loads = [
        pltpu.make_async_copy(head_ref.at[:, pl.ds(t * 128, 128)], hb.at[0, t], load_sem.at[t]) for t in range(TILES - 1)
    ]
    for copy in [hid_load, tail_load] + tile_loads:
        copy.start()

    sent = []

    def go(make):
        make().start()
        sent.append(make)

    def piece(shard, tile, sub):
        return hb.at[shard, tile, pl.ds(sub * SUB, SUB), :]

    def place(d, half):
        return tok.at[pl.ds(PLACE[d] * ROWS + half * HALF, HALF), :]

    def x_copy(side, i, src_shard):
        shard, quarter, sub = X_SEQ[side][i]
        tile = (2 * h + quarter) * 2 + core
        return remote(
            piece(src_shard, tile, sub), piece(shard, tile, sub), xs.at[side, i], xr.at[side, i],
            x_peer(-1 if side == 0 else 1),
        )

    def y_copy(side, i, parity):
        shard, quarter, sub = Y_SEQ[side][i]
        tile = (2 * parity + quarter) * 2 + core
        return remote(
            piece(shard, tile, sub), piece(shard, tile, sub), ys.at[side, i], yr.at[side, i],
            y_peer(-1 if side == 0 else 1),
        )

    def b_copy(kind, i, sender):
        shard, quarter, sub = (X_SEQ + Y_SEQ)[kind][i]
        parity = h if kind < 2 else 1 - h
        tile = (2 * parity + quarter) * 2 + sender
        return remote(piece(shard, tile, sub), piece(shard, tile, sub), bs.at[kind, i], br.at[kind, i], twin)

    def z_copy(side, i, src):
        d, half = Z_SEQ[side][i]
        return remote(
            place(src, half), place(d, half), zs.at[side, i], zr.at[side, i], z_peer(-1 if side == 0 else 1)
        )

    hid_load.wait()
    norm_rows(hid, gain_ref, target_ref, stage)
    tail_load.wait()
    stage7[...] = jnp.concatenate([tail[...], jnp.zeros((D, 128 - LAST), jnp.bfloat16)], axis=1)
    stage_copy = pltpu.make_async_copy(stage, tok.at[pl.ds(own, ROWS), :], load_sem.at[8])
    stage7_copy = pltpu.make_async_copy(stage7, hb.at[0, TILES - 1], load_sem.at[7])
    stage_copy.start()
    stage7_copy.start()
    pl.semaphore_wait(barrier, len(peers))
    stage_copy.wait()
    for i in range(2):
        for side in range(2):
            go(functools.partial(z_copy, side, i, 0))
    for copy in tile_loads:
        copy.wait()
    stage7_copy.wait()
    for i in range(2 * SUBS):
        for side in range(2):
            go(functools.partial(x_copy, side, i, 0))

    def zero(i, carry):
        rows = pl.ds(pl.multiple_of(i * ROWS, ROWS), ROWS)
        for ref in (mx, sm, en, tg):
            ref[rows, :] = jnp.zeros((ROWS, 128), jnp.float32)
        return carry

    lax.fori_loop(0, NZ, zero, 0)
    aim_rows(tok, tb, own, ROWS)

    def got_x(i):
        for side in range(2):
            shard, quarter, sub = X_SEQ[side][i]
            x_copy(side, i, 0).wait_recv()
            go(functools.partial(y_copy, quarter, Y_SEQ[quarter].index((shard, quarter, sub)), h))
            go(functools.partial(b_copy, side, i, core))
            if i < SUBS:
                go(functools.partial(x_copy, side, i + 2 * SUBS, shard))

    def got_y(i):
        for side in range(2):
            y_copy(side, i, 1 - h).wait_recv()
            go(functools.partial(b_copy, 2 + side, i, core))

    def got_tx(i):
        for kind in (0, 1):
            b_copy(kind, i, 1 - core).wait_recv()

    def got_ty(i):
        for kind in (2, 3):
            b_copy(kind, i, 1 - core).wait_recv()

    def got_z(i):
        for side in range(2):
            d, half = Z_SEQ[side][i]
            z_copy(side, i, 0).wait_recv()
            later = i + 2 if i < 4 else 6
            if i < 6 and Z_SEQ[side][later][1] == half:
                go(functools.partial(z_copy, side, later, d))
            aim_rows(tok, tb, PLACE[d] * ROWS + half * HALF, HALF)

    handlers = {"x": got_x, "y": got_y, "tx": got_tx, "ty": got_ty, "z": got_z}
    distance = {at: d for d, at in PLACE.items()}

    def figures_copy(block):
        d = distance[block]
        return remote(stats.at[block], inbox.at[NZ - d], ss.at[d], sr.at[NZ - d], z_peer(d))

    ahead, rest = plan()
    acts = [[functools.partial(handlers[kind], i) for kind, i in events] for events in ahead]
    acts.append([functools.partial(handlers[kind], i) for kind, i in rest])
    for step, blocks in DONE.items():
        for block in blocks:
            acts[step + 1].append(functools.partial(block_stats, mx, sm, en, tg, stats, block))
            acts[min(step + 2, len(STEPS))].append(functools.partial(go, functools.partial(figures_copy, block)))

    def run(i, low, high):
        if not any(acts[low:high]):
            return
        if high - low == 1:
            for act in acts[low]:
                act()
            return
        middle = (low + high) // 2
        if any(acts[low:middle]):
            pl.when(i < middle)(lambda: run(i, low, middle))
        if any(acts[middle:high]):
            pl.when(i >= middle)(lambda: run(i, middle, high))

    def columns_of(pairs):
        units = []
        for p in pairs:
            for shard, k in pair_units(p, h):
                step = jnp.where(shard == 2, 3, jnp.where(shard == 3, 2, shard))
                units.append((shard, k, (((x + step) % NX) * NZ + z) * WIDTH + k * 256))
        return units

    def one(i, carry):
        run(i, 0, len(STEPS))
        kind, rows, columns = packed(i)

        @pl.when(kind == 0)
        def _():
            base = 256 * ((rows - 1) // 2) + HALF * ((rows - 1) % 2)
            low = jnp.where(rows == 0, own, jnp.where(rows == 7, PLACE[4] * ROWS, base))
            step = jnp.where((rows == 0) | (rows == 7), HALF, ROWS)
            spans = [pl.ds(pl.multiple_of(low + j * step, HALF), HALF) for j in range(2)]
            pairs = [jnp.int32(QUADS[0][j]) for j in range(2)]
            for q in range(1, 4):
                pairs = [jnp.where(columns == q, QUADS[q][j], pairs[j]) for j in range(2)]
            compute_step(tok, hb, tb, mx, sm, en, tg, spans, columns_of(pairs), columns == 0)

        @pl.when(kind == 1)
        def _():
            spans = [pl.ds(pl.multiple_of(rows * 256, 256), 256)]
            compute_step(tok, hb, tb, mx, sm, en, tg, spans, columns_of([columns]), None)

        return carry

    lax.fori_loop(0, len(STEPS), one, 0)
    for act in acts[len(STEPS)]:
        act()
    block_stats(mx, sm, en, tg, stats, PLACE[0])
    for d in range(1, NZ):
        remote(stats.at[0], inbox.at[d], ss.at[d], sr.at[d], z_peer(d)).wait_recv()
    all_of = [stats[PLACE[0]]] + [inbox[d] for d in range(1, NZ)]
    top = functools.reduce(jnp.maximum, [part[0:1, :] for part in all_of])
    total = ent = tgt = jnp.zeros((1, ROWS), jnp.float32)
    for part in all_of:
        gap = part[0:1, :] - top
        scale = jnp.exp(gap)
        total += part[1:2, :] * scale
        ent += (part[2:3, :] + gap * part[1:2, :]) * scale
        tgt += part[3:4, :]
    log_total = jnp.log(total)
    out_ref[0:1, :] = tgt - (top + log_total)
    out_ref[1:2, :] = log_total - ent / total
    for make in sent:
        make().wait_send()


def on_device(hidden, gain, head, lengths, mask, targets):
    rows = hidden.shape[0]
    me = lax.axis_index("tp")
    vm = pltpu.VMEM
    dma = pltpu.SemaphoreType.DMA
    stat = vm((NZ * ROWS, 128), jnp.float32)
    small = vm((NZ, 8, 128), jnp.float32)
    anywhere, near = pl.BlockSpec(memory_space=pl.ANY), pl.BlockSpec(memory_space=pltpu.VMEM)
    out = pl.pallas_call(
        kernel,
        out_shape=jax.ShapeDtypeStruct((8, ROWS), jnp.float32),
        in_specs=[anywhere, near, near, anywhere],
        out_specs=near,
        scratch_shapes=[
            vm((D, ROWS), jnp.bfloat16),
            vm((ROWS, DE), jnp.bfloat16),
            vm((D, LAST), jnp.bfloat16),
            vm((D, 128), jnp.bfloat16),
            vm((NZ * ROWS, DE), jnp.bfloat16),
            vm((NX, TILES, D, 128), jnp.bfloat16),
            stat, stat, stat, stat, stat,
            small, small,
            dma((9,)),
            dma((2, 3 * SUBS)), dma((2, 3 * SUBS)),
            dma((2, 3 * SUBS)), dma((2, 3 * SUBS)),
            dma((2, 7)), dma((2, 7)),
            dma((4, 3 * SUBS)), dma((4, 3 * SUBS)),
            dma((NZ,)), dma((NZ,)),
        ],
        compiler_params=pltpu.CompilerParams(
            collective_id=0, has_side_effects=True, vmem_limit_bytes=62 << 20
        ),
    )(hidden.T, gain.reshape(1, D), targets.reshape(1, rows), head)
    row_ids = me * rows + jnp.arange(rows, dtype=jnp.int32)
    slot = row_ids % SEQ_LEN
    seq_id = row_ids // SEQ_LEN
    match = seq_id[:, None] == jnp.arange(lengths.shape[0], dtype=jnp.int32)[None, :]
    seq_len = jnp.sum(jnp.where(match, lengths[None, :], 0), axis=1)
    valid = (slot < seq_len) & (mask == 1)
    return (jnp.where(valid, out[0], 0.0), jnp.where(valid, out[1], 0.0))


def solution(mesh):
    return jax.shard_map(
        on_device,
        mesh=mesh,
        in_specs=(
            P(("dp", "tp"), None),
            P(),
            P(None, "tp"),
            P("dp"),
            P(("dp", "tp")),
            P(("dp", "tp")),
        ),
        out_specs=(P(("dp", "tp")), P(("dp", "tp"))),
        check_vma=False,
    )
```

time: 457 us -> 70.9 us (0.16)
  the two profiles are of different devices: /device:TPU:8 before, /device:TPU:1 now
where the time goes in v2:
time: 70.9 us; the launch traced here: 70.6 us
  Pallas kernels  66.2 us (93%)
  other arithmetic  2.47 us (3%)
  local copies, waits for them, and re-layouts  1.3 us (2%)
    pallas_call x1, Pallas kernels, on_device(): pl.pallas_call(kernel, out_shape=jax.ShapeDtypeStruct((8, ROWS), jnp.floa...  66.2 us
    select_n x2, other arithmetic, on_device(): return (jnp.where(valid, out[0], 0.0), jnp.where(valid, out[1], 0.0))  2.38 us

profile of v2, /device:TPU:1, one launch (start us, length us, event | category | flops | bytes accessed | tf_op | source)
XLA Modules:
  0.0 70.6 jit_solution(7176221454864117466)
XLA Ops:
  0.6 0.0 copy-start.1
  0.6 0.0 copy-start
  0.7 1.3 %reshape.30.gain_ref = bf16[1,1600]{1,0:T(2,128)(2,1)} reshape(bf16[1600]{0:T(1024)(128)(2,1)} %param.7) | data formatting | bytes 6400 | tf_op jit(solution)/shard_map/reshape | solution.py:453
  1.9 66.2 %shard_map.77 = f32[8,128]{1,0:T(8,128)} custom-call(bf16[1600,128]{1,0:T(8,128)(2,1)} %bitcast.6, bf16[1,1600]{1,0:T(2,128)(2,1)} %reshape.30.gain_ref, s32[1,128]{1,0:T(1,128)} %bitcast.7, bf16[1600,1000]{1,0:T(8,128)(2,1)} %head_ref.1), custom_call_target="tpu_custom_call" | custom-call | tf_op jit(solution)/shard_map/pallas_call | solution.py:429
  68.1 0.0 copy-done.1
  68.1 0.1 select_reduce_fusion
  68.2 0.0 copy-done
  68.2 1.2 %bitcast_select_fusion = (f32[128]{0:T(128)}, pred[128]{0:T(512)(128)(4,1)S(1)}) fusion(f32[8,128]{1,0:T(8,128)} %shard_map.77, s32[128]{0:T(128)S(1)} %copy-done, s32[128]{0:T(128)S(1)} %select_reduce_fusion, s32[]{:T(128)S(6)} %mul.3), kind=kLoop, calls=%fused_computation.8 | loop fusion | flops 2048 | bytes 2180 | tf_op jit(solution)/shard_map/jit(_where)/select_n | solution.py:460
  69.4 1.2 %bitcast_select_fusion.1 = f32[128]{0:T(128)} fusion(pred[128]{0:T(512)(128)(4,1)S(1)} %get-tuple-element.3, f32[8,128]{1,0:T(8,128)} %shard_map.77), kind=kLoop, calls=%fused_computation.9 | loop fusion | flops 128 | bytes 1152 | tf_op jit(solution)/shard_map/jit(_where)/select_n | solution.py:460
  (1 shorter events, 0.0 us)
Async XLA Ops:
  0.6 67.5 %copy-start.1 = (s32[16]{0:T(128)S(1)}, s32[16]{0:T(128)}, u32[]{:S(2)}) copy-start(s32[16]{0:T(128)} %param.9) | copy-start | bytes 196
  0.6 67.6 %copy-start = (s32[128]{0:T(128)S(1)}, s32[128]{0:T(128)}, u32[]{:S(2)}) copy-start(s32[128]{0:T(128)} %param.10) | copy-start | bytes 1540
